TPU v7x, 512 devices: a whole 4x4x16 slice. The times are simulated.
512 devices in a mesh: dp: 4 (over x), expert: 128 (over z, y, core).
Axes of the slice: x: 4, y: 4, z: 16, core: 2. Of those that a mesh axis runs over, the one named last changes fastest.
Arguments:
- tokens: bfloat16 [65536, 2048], P(('dp', 'expert')), may hold values from -6 to 6
- hidden_grad: bfloat16 [65536, 1, 768], P(('dp', 'expert')), may hold values from -6 to 6
- gate_prob: float32 [65536, 1], P(('dp', 'expert')), may hold values from 0.2 to 1
- slot_choice: int32 [65536, 1], P(('dp', 'expert')), may hold values from 0 to 127; in each aligned block of 128 rows (0 to 127, 128 to 255, ...) at most 2 rows name the same one
- replica_plan: int32 [128], replicated, may hold values from 0 to 63, as said below
- weights: bfloat16 [64, 2, 2048, 768], P(None, None, ('dp', 'expert')), may hold values from -0.125 to 0.125
Outputs:
- input_grad: bfloat16 [65536, 2048], P(('dp', 'expert'))
- expert_grad: bfloat16 [64, 2, 2048, 768], P(None, None, ('dp', 'expert'))
Inputs may be any that keep to these rules, and one draw needn't show every extreme that they name: `slot_choice`: among the tokens of one device no slot is named more than 2 times, and 2 is reached; the picks of one token name different slots. `replica_plan`: every expert is held by at least one slot.
All inputs are finite; a program needn't handle non-finite values.
Results may differ from a plain program's by a relative error of at most 0.007.
Values may be sent and summed in bfloat16 or wider, within the bound.
A program may use at most 64 MiB of HBM per device.

v0:
```python
import jax
import jax.numpy as jnp
from jax import lax
from jax.sharding import PartitionSpec as P


def back_project(grad_gate, grad_up, weight_pair):
    contract_cols = (((1,), (1,)), ((), ()))
    first_term = lax.dot_general(
        grad_gate, weight_pair[0], contract_cols, preferred_element_type=jnp.float32
    )
    return first_term + lax.dot_general(
        grad_up, weight_pair[1], contract_cols, preferred_element_type=jnp.float32
    )


def row_products(inputs, grad_gate, grad_up):
    contract_rows = (((0,), (0,)), ((), ()))
    return jnp.stack(
        [
            lax.dot_general(inputs, grad_gate, contract_rows, preferred_element_type=jnp.float32),
            lax.dot_general(inputs, grad_up, contract_rows, preferred_element_type=jnp.float32),
        ]
    )


def per_device(tokens, hidden_grad, gate_prob, slot_choice, replica_plan, weights):
    expert_count = lax.axis_size("expert")
    group_count = lax.axis_size("dp")
    token_count, pick_count = slot_choice.shape
    row_count = token_count * pick_count
    capacity = max(2, 2 * row_count // expert_count)
    depth_rows = expert_count * capacity
    model_width = tokens.shape[1]
    hidden_width = hidden_grad.shape[2]
    expert_total = weights.shape[0]
    shard_rows = weights.shape[2]
    block_rows = shard_rows * expert_count
    flat_slot = slot_choice.reshape(row_count)
    slot_member = (flat_slot[:, None] == jnp.arange(expert_count, dtype=jnp.int32)[None, :]).astype(
        jnp.int32
    )
    ranking = jnp.sum((jnp.cumsum(slot_member, axis=0) - 1) * slot_member, axis=1)
    position = flat_slot * capacity + ranking
    scatter_table = (jnp.arange(depth_rows, dtype=jnp.int32)[:, None] == position[None, :]).astype(
        jnp.bfloat16
    )
    token_rows = jnp.repeat(tokens, pick_count, axis=0)
    cotangent = (gate_prob[:, :, None] * hidden_grad.astype(jnp.float32)).astype(jnp.bfloat16)
    cotangent = cotangent.reshape(row_count, hidden_width)
    send_inputs = jnp.dot(scatter_table, token_rows, preferred_element_type=jnp.float32).astype(
        jnp.bfloat16
    )
    send_cotangent = jnp.dot(scatter_table, cotangent, preferred_element_type=jnp.float32).astype(
        jnp.bfloat16
    )
    recv_inputs, recv_cotangent = (
        lax.all_to_all(
            send_inputs.reshape(expert_count, capacity, model_width),
            "expert",
            split_axis=0,
            concat_axis=0,
            tiled=True,
        ),
        lax.all_to_all(
            send_cotangent.reshape(expert_count, capacity, hidden_width),
            "expert",
            split_axis=0,
            concat_axis=0,
            tiled=True,
        ),
    )
    recv_inputs = recv_inputs.reshape(depth_rows, model_width)
    recv_cotangent = recv_cotangent.reshape(depth_rows, hidden_width)
    chooser = (replica_plan[:, None] == jnp.arange(expert_total, dtype=jnp.int32)[None, :]).astype(
        jnp.bfloat16
    )
    send_weights = jnp.einsum(
        "se,ekdf->skdf", chooser, weights, preferred_element_type=jnp.float32
    ).astype(jnp.bfloat16)
    own_weights = lax.all_to_all(
        send_weights, "expert", split_axis=0, concat_axis=2, tiled=True
    ).reshape(2, block_rows, hidden_width)
    piece = lax.all_gather(own_weights, "dp", axis=1, tiled=True)
    gate_sum = jnp.dot(recv_inputs, piece[0], preferred_element_type=jnp.float32)
    up_sum = jnp.dot(recv_inputs, piece[1], preferred_element_type=jnp.float32)
    sigma = jax.nn.sigmoid(gate_sum)
    scaled = recv_cotangent.astype(jnp.float32)
    grad_gate = (scaled * up_sum * sigma * (1.0 + gate_sum * (1.0 - sigma))).astype(jnp.bfloat16)
    grad_up = (scaled * gate_sum * sigma).astype(jnp.bfloat16)
    all_gate, all_up = (
        lax.all_gather(grad_gate, "dp", axis=0, tiled=True),
        lax.all_gather(grad_up, "dp", axis=0, tiled=True),
    )
    split_inputs = recv_inputs.reshape(depth_rows, group_count, block_rows)
    all_columns = lax.all_to_all(
        split_inputs, "dp", split_axis=1, concat_axis=0, tiled=True
    ).reshape(group_count * depth_rows, block_rows)
    row_terms = back_project(all_gate, all_up, own_weights).astype(jnp.bfloat16)
    summed = jnp.zeros((2, block_rows, hidden_width), jnp.float32)
    for group_index in range(group_count):
        lower = group_index * depth_rows
        upper = lower + depth_rows
        products = row_products(
            all_columns[lower:upper], all_gate[lower:upper], all_up[lower:upper]
        )
        summed = summed + lax.optimization_barrier(products.astype(jnp.bfloat16)).astype(
            jnp.float32
        )
    pieces = summed.reshape(2, expert_count, shard_rows, hidden_width)
    gathered = lax.all_to_all(
        pieces.astype(jnp.bfloat16), "expert", split_axis=1, concat_axis=1, tiled=True
    ).astype(pieces.dtype)
    membership = (
        jnp.arange(expert_total, dtype=jnp.int32)[:, None] == replica_plan[None, :]
    ).astype(jnp.float32)
    expert_grad = jnp.einsum("es,ksdf->ekdf", membership, gathered, precision=lax.Precision.HIGHEST)
    expert_grad = (expert_grad / group_count).astype(jnp.bfloat16)
    joined = lax.all_to_all(
        row_terms.reshape(group_count, depth_rows, block_rows),
        "dp",
        split_axis=0,
        concat_axis=2,
        tiled=True,
    )
    back_rows = lax.all_to_all(
        joined.reshape(expert_count, capacity, model_width),
        "expert",
        split_axis=0,
        concat_axis=0,
        tiled=True,
    )
    back_rows = back_rows.reshape(depth_rows, model_width)
    token_grads = lax.dot_general(
        scatter_table, back_rows, (((0,), (0,)), ((), ())), preferred_element_type=jnp.float32
    )
    input_grad = jnp.sum(token_grads.reshape(token_count, pick_count, model_width), axis=1).astype(
        jnp.bfloat16
    )
    return (input_grad, expert_grad)


def solution(mesh):
    placed = (
        P(("dp", "expert"), None),
        P(("dp", "expert"), None, None),
        P(("dp", "expert"), None),
        P(("dp", "expert"), None),
        P(),
        P(None, None, ("dp", "expert"), None),
    )
    return jax.shard_map(
        per_device,
        mesh=mesh,
        in_specs=placed,
        out_specs=(P(("dp", "expert"), None), P(None, None, ("dp", "expert"), None)),
        check_vma=False,
    )
```

profile of v0, /device:TPU:33, one launch (start us, length us, event | category | flops | bytes accessed | tf_op | source)
XLA Modules:
  0.0 494.8 jit_solution(11595988162404496423)
XLA Ops:
  7.2 1.1 copy-done
  8.3 1.3 convolution_convert_fusion.2
  9.6 1.2 copy.26
  10.8 96.8 %all_to_all.65 = bf16[128,2,4,768]{3,2,1,0:T(4,128)(2,1)S(1)} all-to-all(bf16[128,2,4,768]{3,2,1,0:T(4,128)(2,1)S(1)} %copy.26), channel_id=1, replica_groups=mesh['dp'=4,'expert'=128] {'expert'}, dimensions={0} | all-to-all | bytes 3145728 | tf_op jit(solution)/shard_map/all_to_all | solution.py:81
  107.6 2.4 copy.27
  110.0 0.6 copy-done.7
  111.4 0.9 reshape.66
  112.3 7.0 %all-to-all-start = ((bf16[128,2,768]{2,1,0:T(2,128)(2,1)}), bf16[128,2,768]{2,1,0:T(2,128)(2,1)S(1)}, u32[]{:S(2)}, u32[]{:S(2)}) async-start(bf16[128,2,768]{2,1,0:T(2,128)(2,1)} %reshape.66), calls=%async_computation | async-start | bytes 786432 | tf_op jit(solution)/shard_map/all_to_all | solution.py:65
  119.4 1.5 convolution_convert_fusion
  120.9 1.6 reshape.67
  122.5 25.1 %all-to-all-done = bf16[128,2,768]{2,1,0:T(2,128)(2,1)S(1)} async-done(((bf16[128,2,768]{2,1,0:T(2,128)(2,1)}), bf16[128,2,768]{2,1,0:T(2,128)(2,1)S(1)}, u32[]{:S(2)}, u32[]{:S(2)}) %all-to-all-start) | async-done | bytes 393248 | tf_op jit(solution)/shard_map/all_to_all | solution.py:65
  147.6 6.1 %all-to-all-start.1 = ((bf16[128,2,2048]{2,1,0:T(2,128)(2,1)}), bf16[128,2,2048]{2,1,0:T(2,128)(2,1)S(1)}, u32[]{:S(2)}, u32[]{:S(2)}) async-start(bf16[128,2,2048]{2,1,0:T(2,128)(2,1)} %reshape.67), calls=%async_computation.1 | async-start | bytes 2097152 | tf_op jit(solution)/shard_map/all_to_all | solution.py:58
  153.9 1.0 reshape.73
  154.9 54.4 %all-to-all-done.1 = bf16[128,2,2048]{2,1,0:T(2,128)(2,1)S(1)} async-done(((bf16[128,2,2048]{2,1,0:T(2,128)(2,1)}), bf16[128,2,2048]{2,1,0:T(2,128)(2,1)S(1)}, u32[]{:S(2)}, u32[]{:S(2)}) %all-to-all-start.1) | async-done | bytes 1048608 | tf_op jit(solution)/shard_map/all_to_all | solution.py:58
  209.3 1.3 reshape.68
  210.6 12.7 %fusion.40 = (bf16[1,2048,768]{2,0,1:T(2,128)(2,1)S(1)}, bf16[1,2048,768]{2,0,1:T(2,128)(2,1)S(1)}) fusion(bf16[2,2048,768]{2,0,1:T(2,128)(2,1)} %all-gather.4.cloned.1.call-done), kind=kLoop, calls=%fused_computation.69 | loop fusion | bytes 12582912 | tf_op jit(solution)/shard_map/slice | solution.py:85
  223.3 1.8 multiply_convert_fusion.1
  225.1 1.9 fusion.17
  227.1 0.7 all-gather.8.cloned.1.call-update
  227.8 1.4 fusion.41
  229.2 1.6 squeeze.15
  230.9 21.3 %all-gather.6.cloned.1.call-done = bf16[1024,768]{1,0:T(8,128)(2,1)} async-done(((bf16[256,768]{1,0:T(8,128)(2,1)}), bf16[1024,768]{1,0:T(8,128)(2,1)}) %all-gather.6.cloned.1.call-update) | async-done | bytes 1572880 | tf_op jit(solution)/shard_map/all_gather | solution.py:92
  252.3 3.8 fusion.42
  256.0 33.1 %all-gather.8.cloned.1.call-done = bf16[1024,768]{1,0:T(8,128)(2,1)} async-done(((bf16[256,768]{1,0:T(8,128)(2,1)}), bf16[1024,768]{1,0:T(8,128)(2,1)}) %all-gather.8.cloned.1.call-update) | async-done | bytes 1572880 | tf_op jit(solution)/shard_map/all_gather | solution.py:93
  289.1 4.1 add_convert_fusion.1
  293.2 3.5 all-to-all-start.3
  296.7 1.5 reshape_reshape.3
  298.2 2.4 copy.31
  300.6 10.4 %all-to-all-done.3 = bf16[4,256,512]{2,1,0:T(8,128)(2,1)S(1)} async-done(((bf16[4,256,512]{2,1,0:T(8,128)(2,1)}), bf16[4,256,512]{2,1,0:T(8,128)(2,1)S(1)}, u32[]{:S(2)}, u32[]{:S(2)}) %all-to-all-start.3) | async-done | bytes 1048608 | tf_op jit(solution)/shard_map/all_to_all | solution.py:119
  311.0 3.5 all-to-all-start.5
  314.6 1.8 copy.30
  316.3 2.3 reshape.71
  318.6 9.4 %all-to-all-done.5 = bf16[256,4,512]{2,0,1:T(8,128)(2,1)S(1)} async-done(((bf16[256,4,512]{2,0,1:T(8,128)(2,1)}), bf16[256,4,512]{2,0,1:T(8,128)(2,1)S(1)}, u32[]{:S(2)}, u32[]{:S(2)}) %all-to-all-start.5) | async-done | bytes 1048608 | tf_op jit(solution)/shard_map/all_to_all | solution.py:96
  328.0 18.6 %all-to-all-start.4 = ((bf16[128,2,2048]{2,1,0:T(2,128)(2,1)}), bf16[128,2,2048]{2,1,0:T(2,128)(2,1)S(1)}, u32[]{:S(2)}, u32[]{:S(2)}) async-start(bf16[128,2,2048]{2,1,0:T(2,128)(2,1)} %reshape.71), calls=%async_computation.4 | async-start | bytes 2097152 | tf_op jit(solution)/shard_map/all_to_all | solution.py:126
  346.6 1.4 fusion.12
  348.0 1.4 fusion.13
  349.6 1.2 copy-done.2
  351.9 0.4 fusion.6
  353.9 2.0 add_convert_fusion
  355.8 2.9 convert_element_type.82
  358.7 1.7 copy.32
  360.4 41.8 %all-to-all-done.4 = bf16[128,2,2048]{2,1,0:T(2,128)(2,1)S(1)} async-done(((bf16[128,2,2048]{2,1,0:T(2,128)(2,1)}), bf16[128,2,2048]{2,1,0:T(2,128)(2,1)S(1)}, u32[]{:S(2)}, u32[]{:S(2)}) %all-to-all-start.4) | async-done | bytes 1048608 | tf_op jit(solution)/shard_map/all_to_all | solution.py:126
  402.2 6.5 %all-to-all-start.6 = ((bf16[2,128,4,768]{3,2,0,1:T(4,128)(2,1)}), bf16[2,128,4,768]{3,2,0,1:T(4,128)(2,1)S(1)}, u32[]{:S(2)}, u32[]{:S(2)}) async-start(bf16[2,128,4,768]{3,2,0,1:T(4,128)(2,1)} %copy.32), calls=%async_computation.6 | async-start | bytes 3145728 | tf_op jit(solution)/shard_map/all_to_all | solution.py:111
  408.7 1.2 reshape.72
  410.0 2.4 convolution_convert_fusion.1
  412.4 73.8 %all-to-all-done.6 = bf16[2,128,4,768]{3,2,0,1:T(4,128)(2,1)S(1)} async-done(((bf16[2,128,4,768]{3,2,0,1:T(4,128)(2,1)}), bf16[2,128,4,768]{3,2,0,1:T(4,128)(2,1)S(1)}, u32[]{:S(2)}, u32[]{:S(2)}) %all-to-all-start.6) | async-done | bytes 1572896 | tf_op jit(solution)/shard_map/all_to_all | solution.py:111
  486.2 0.5 multiply_convert_fusion
  486.8 1.5 copy.34
  (38 shorter events, 4.0 us)
Async XLA Ops:
  7.2 1.1 copy-start
  7.2 203.4 %all-gather.4.cloned.1.call-start = ((), (), s32[]{:S(2)}) async-start(), calls=%async_computation.7 | async-start | bytes 7864320 | tf_op jit(solution)/shard_map/all_gather | solution.py:84
  110.0 0.7 copy-start.7
  110.0 1.1 copy-start.6
  110.0 1.1 copy-start.9
  112.3 35.2 %all-to-all-start = ((bf16[128,2,768]{2,1,0:T(2,128)(2,1)}), bf16[128,2,768]{2,1,0:T(2,128)(2,1)S(1)}, u32[]{:S(2)}, u32[]{:S(2)}) async-start(bf16[128,2,768]{2,1,0:T(2,128)(2,1)} %reshape.66), calls=%async_computation | async-start | bytes 786432 | tf_op jit(solution)/shard_map/all_to_all | solution.py:65
  147.6 61.7 %all-to-all-start.1 = ((bf16[128,2,2048]{2,1,0:T(2,128)(2,1)}), bf16[128,2,2048]{2,1,0:T(2,128)(2,1)S(1)}, u32[]{:S(2)}, u32[]{:S(2)}) async-start(bf16[128,2,2048]{2,1,0:T(2,128)(2,1)} %reshape.67), calls=%async_computation.1 | async-start | bytes 2097152 | tf_op jit(solution)/shard_map/all_to_all | solution.py:58
  153.7 98.6 %all-gather.6.cloned.1.call-start = ((), (), s32[]{:S(2)}) async-start(), calls=%async_computation.8 | async-start | bytes 1966080 | tf_op jit(solution)/shard_map/all_gather | solution.py:92
  210.6 12.7 %copy-start.5 = (f32[256,768]{1,0:T(8,128)S(1)}, f32[256,768]{1,0:T(8,128)}, u32[]{:S(2)}) copy-start(f32[256,768]{1,0:T(8,128)} %reshape.73) | copy-start | bytes 2359300
  210.6 12.7 %copy-start.4 = (bf16[256,2048]{1,0:T(8,128)(2,1)S(1)}, bf16[256,2048]{1,0:T(8,128)(2,1)}, u32[]{:S(2)}) copy-start(bf16[256,2048]{1,0:T(8,128)(2,1)} %reshape.68) | copy-start | bytes 3145732
  227.0 62.1 %all-gather.8.cloned.1.call-start = ((), (), s32[]{:S(2)}) async-start(), calls=%async_computation.9 | async-start | bytes 1966080 | tf_op jit(solution)/shard_map/all_gather | solution.py:93
  293.2 17.8 %all-to-all-start.3 = ((bf16[4,256,512]{2,1,0:T(8,128)(2,1)}), bf16[4,256,512]{2,1,0:T(8,128)(2,1)S(1)}, u32[]{:S(2)}, u32[]{:S(2)}) async-start(bf16[4,256,512]{2,1,0:T(8,128)(2,1)} %bitcast.99), calls=%async_computation.3 | async-start | bytes 2097152 | tf_op jit(solution)/shard_map/all_to_all | solution.py:119
  311.0 17.0 %all-to-all-start.5 = ((bf16[256,4,512]{2,0,1:T(8,128)(2,1)}), bf16[256,4,512]{2,0,1:T(8,128)(2,1)S(1)}, u32[]{:S(2)}, u32[]{:S(2)}) async-start(bf16[256,4,512]{2,0,1:T(8,128)(2,1)} %copy.31), calls=%async_computation.5 | async-start | bytes 2097152 | tf_op jit(solution)/shard_map/all_to_all | solution.py:96
  328.0 74.2 %all-to-all-start.4 = ((bf16[128,2,2048]{2,1,0:T(2,128)(2,1)}), bf16[128,2,2048]{2,1,0:T(2,128)(2,1)S(1)}, u32[]{:S(2)}, u32[]{:S(2)}) async-start(bf16[128,2,2048]{2,1,0:T(2,128)(2,1)} %reshape.71), calls=%async_computation.4 | async-start | bytes 2097152 | tf_op jit(solution)/shard_map/all_to_all | solution.py:126
  349.5 1.4 copy-start.2
  349.5 1.9 copy-start.3
  402.2 84.0 %all-to-all-start.6 = ((bf16[2,128,4,768]{3,2,0,1:T(4,128)(2,1)}), bf16[2,128,4,768]{3,2,0,1:T(4,128)(2,1)S(1)}, u32[]{:S(2)}, u32[]{:S(2)}) async-start(bf16[2,128,4,768]{3,2,0,1:T(4,128)(2,1)} %copy.32), calls=%async_computation.6 | async-start | bytes 3145728 | tf_op jit(solution)/shard_map/all_to_all | solution.py:111
  408.7 77.5 %copy-start.8 = (s32[128]{0:T(128)S(1)}, s32[128]{0:T(128)}, u32[]{:S(2)}) copy-start(s32[128]{0:T(128)} %param.10) | copy-start | bytes 1540
  410.0 78.3 %copy-start.1 = (bf16[64,2,4,768]{3,2,1,0:T(4,128)(2,1)S(1)}, bf16[64,2,4,768]{3,2,1,0:T(4,128)(2,1)}, u32[]{:S(2)}) copy-start(bf16[64,2,4,768]{3,2,1,0:T(4,128)(2,1)} %param.11) | copy-start | bytes 2359300
Sparse Core Ops, SparseCore 0:
  110.1 64.8 all-gather.3
  227.1 25.0 all-gather.5
  254.9 34.1 all-gather.7
where the time goes:
time: 496 us; the launch traced here: 495 us
  waiting for transfers between devices  270 us (54%)
  blocking collectives  96.8 us (20%)
  starting transfers between devices  45.6 us (9%)
  local copies, waits for them, and re-layouts  42.5 us (9%)
  matrix products  22.8 us (5%)
  between operations  14 us (3%)
    all_to_all x1, blocking collectives, per_device(): lax.all_to_all(send_weights, 'expert', split_axis=0, concat_axis=2, tiled...  96.8 us
    all_to_all x1, waiting for transfers between devices, per_device(): lax.all_to_all(pieces.astype(jnp.bfloat16), 'expert', split_axis=1, conca...  73.8 us
    all_to_all x1, waiting for transfers between devices, per_device(): lax.all_to_all(send_inputs.reshape(expert_count, capacity, model_width),...  54.4 us
    all_to_all x1, waiting for transfers between devices, per_device(): lax.all_to_all(joined.reshape(expert_count, capacity, model_width), 'expe...  41.8 us
    all_gather x1, waiting for transfers between devices, per_device(): lax.all_gather(grad_up, 'dp', axis=0, tiled=True)  33.1 us
    all_to_all x1, waiting for transfers between devices, per_device(): lax.all_to_all(send_cotangent.reshape(expert_count, capacity, hidden_widt...  25.1 us
    all_gather x1, waiting for transfers between devices, per_device(): lax.all_gather(grad_gate, 'dp', axis=0, tiled=True)  21.3 us
    all_to_all x1, starting transfers between devices, per_device(): lax.all_to_all(joined.reshape(expert_count, capacity, model_width), 'expe...  18.6 us
  transfers between devices with their start and end apart: 9, of which 8 were waited for; matrix products, arithmetic and copies ran while one was open for 8% of the time, Pallas kernels for 0%

commit v1 on v0

--- a/solution.py
+++ b/solution.py
@@ -2,6 +2,28 @@
 import jax.numpy as jnp
 from jax import lax
 from jax.sharding import PartitionSpec as P
+
+
+def in_order(parts, dim):
+    dims = list(parts.shape[1:])
+    dims[dim] *= parts.shape[0]
+    return jnp.moveaxis(parts, 0, dim).reshape(dims)
+
+
+def ring_gather(array, axis, dim):
+    size = lax.axis_size(axis)
+    pairs = [(i, (i + 1) % size) for i in range(size)]
+    back = [(b, a) for a, b in pairs]
+    lower, upper = ([], [])
+    for hop in range(size - 1):
+        if hop % 2 == 0:
+            lower.append(lax.ppermute(lower[-1] if lower else array, axis, pairs))
+        else:
+            upper.append(lax.ppermute(upper[-1] if upper else array, axis, back))
+    blocks = jnp.stack([*lower[::-1], array, *upper])
+    shift = lax.axis_index(axis) - len(lower)
+    blocks = blocks[(jnp.arange(size) - shift) % size]
+    return in_order(blocks, dim)
 
 
 def back_project(grad_gate, grad_up, weight_pair):
@@ -90,7 +112,7 @@
     grad_up = (scaled * gate_sum * sigma).astype(jnp.bfloat16)
     all_gate, all_up = (
         lax.all_gather(grad_gate, "dp", axis=0, tiled=True),
-        lax.all_gather(grad_up, "dp", axis=0, tiled=True),
+        ring_gather(grad_up, "dp", 0),
     )
     split_inputs = recv_inputs.reshape(depth_rows, group_count, block_rows)
     all_columns = lax.all_to_all(

time: 496 us -> 467 us (0.942)
  waiting for transfers between devices: 270 us -> 239 us
  matrix products: 22.8 us -> 16.3 us
    all_gather x1 -> x0, waiting for transfers between devices: 33.1 us -> none  [per_device(): lax.all_gather(grad_up, 'dp', axis=0, tiled=True)]
    all_gather x1, waiting for transfers between devices: 21.3 us -> 0.01 us  [per_device(): lax.all_gather(grad_gate, 'dp', axis=0, tiled=True)]
    ppermute x0 -> x3, waiting for transfers between devices: none -> 20.6 us  [the longest x2 20.6 us: ring_gather(): lower.append(lax.ppermute(lower[-1] if lower else array, axis, pairs))]
    ppermute x0 -> x3, starting transfers between devices: none -> 9.35 us  [the longest x2 5.98 us: ring_gather(): lower.append(lax.ppermute(lower[-1] if lower else array, axis, pairs))]
    all_to_all x1, starting transfers between devices: 18.6 us -> 13 us  [per_device(): lax.all_to_all(joined.reshape(expert_count, capacity, model_width), 'expe...]
  transfers between devices with their start and end apart: 9 -> 11, of which waited for: 8 -> 8; matrix products, arithmetic and copies ran while one was open for 8% -> 8% of each run, Pallas kernels for 0% -> 0%
where the time goes in v1:
time: 467 us; the launch traced here: 466 us
  waiting for transfers between devices  239 us (51%)
  blocking collectives  96.8 us (21%)
  starting transfers between devices  49.3 us (11%)
  local copies, waits for them, and re-layouts  45.7 us (10%)
  matrix products  16.3 us (3%)
  between operations  14.4 us (3%)
    all_to_all x1, blocking collectives, per_device(): lax.all_to_all(send_weights, 'expert', split_axis=0, concat_axis=2, tiled...  96.8 us
    all_to_all x1, waiting for transfers between devices, per_device(): lax.all_to_all(pieces.astype(jnp.bfloat16), 'expert', split_axis=1, conca...  74.9 us
    all_to_all x1, waiting for transfers between devices, per_device(): lax.all_to_all(send_inputs.reshape(expert_count, capacity, model_width),...  54.4 us
    all_to_all x1, waiting for transfers between devices, per_device(): lax.all_to_all(joined.reshape(expert_count, capacity, model_width), 'expe...  44.1 us
    all_to_all x1, waiting for transfers between devices, per_device(): lax.all_to_all(send_cotangent.reshape(expert_count, capacity, hidden_widt...  25.1 us
    ppermute x2, waiting for transfers between devices, ring_gather(): lower.append(lax.ppermute(lower[-1] if lower else array, axis, pairs))  20.6 us
    all_to_all x1, starting transfers between devices, per_device(): lax.all_to_all(joined.reshape(expert_count, capacity, model_width), 'expe...  13 us
    slice x1, local copies, waits for them, and re-layouts, per_device(): piece[0]  12.7 us
  transfers between devices with their start and end apart: 11, of which 8 were waited for; matrix products, arithmetic and copies ran while one was open for 8% of the time, Pallas kernels for 0%

profile of v1, /device:TPU:33, one launch (start us, length us, event | category | flops | bytes accessed | tf_op | source)
XLA Modules:
  0.0 465.9 jit_solution(16628256253140691697)
XLA Ops:
  7.2 1.1 copy-done
  8.3 1.3 convolution_convert_fusion.2
  9.6 1.2 copy.26
  10.8 96.8 %all_to_all.65 = bf16[128,2,4,768]{3,2,1,0:T(4,128)(2,1)S(1)} all-to-all(bf16[128,2,4,768]{3,2,1,0:T(4,128)(2,1)S(1)} %copy.26), channel_id=1, replica_groups=mesh['dp'=4,'expert'=128] {'expert'}, dimensions={0} | all-to-all | bytes 3145728 | tf_op jit(solution)/shard_map/all_to_all | solution.py:103
  107.6 2.4 copy.27
  111.4 0.9 reshape.122
  112.3 7.0 %all-to-all-start = ((bf16[128,2,768]{2,1,0:T(2,128)(2,1)}), bf16[128,2,768]{2,1,0:T(2,128)(2,1)S(1)}, u32[]{:S(2)}, u32[]{:S(2)}) async-start(bf16[128,2,768]{2,1,0:T(2,128)(2,1)} %reshape.122), calls=%async_computation | async-start | bytes 786432 | tf_op jit(solution)/shard_map/all_to_all | solution.py:87
  119.4 1.5 convolution_convert_fusion
  120.9 1.6 reshape.123
  122.5 25.1 %all-to-all-done = bf16[128,2,768]{2,1,0:T(2,128)(2,1)S(1)} async-done(((bf16[128,2,768]{2,1,0:T(2,128)(2,1)}), bf16[128,2,768]{2,1,0:T(2,128)(2,1)S(1)}, u32[]{:S(2)}, u32[]{:S(2)}) %all-to-all-start) | async-done | bytes 393248 | tf_op jit(solution)/shard_map/all_to_all | solution.py:87
  147.5 6.1 %all-to-all-start.1 = ((bf16[128,2,2048]{2,1,0:T(2,128)(2,1)}), bf16[128,2,2048]{2,1,0:T(2,128)(2,1)S(1)}, u32[]{:S(2)}, u32[]{:S(2)}) async-start(bf16[128,2,2048]{2,1,0:T(2,128)(2,1)} %reshape.123), calls=%async_computation.1 | async-start | bytes 2097152 | tf_op jit(solution)/shard_map/all_to_all | solution.py:80
  153.9 1.0 reshape.130
  154.9 54.4 %all-to-all-done.1 = bf16[128,2,2048]{2,1,0:T(2,128)(2,1)S(1)} async-done(((bf16[128,2,2048]{2,1,0:T(2,128)(2,1)}), bf16[128,2,2048]{2,1,0:T(2,128)(2,1)S(1)}, u32[]{:S(2)}, u32[]{:S(2)}) %all-to-all-start.1) | async-done | bytes 1048608 | tf_op jit(solution)/shard_map/all_to_all | solution.py:80
  209.3 1.3 reshape.124
  210.5 12.7 %fusion.38 = (bf16[1,2048,768]{2,0,1:T(2,128)(2,1)S(1)}, bf16[1,2048,768]{2,0,1:T(2,128)(2,1)S(1)}) fusion(bf16[2,2048,768]{2,0,1:T(2,128)(2,1)} %all-gather.3.cloned.1.call-done), kind=kLoop, calls=%fused_computation.78 | loop fusion | bytes 12582912 | tf_op jit(solution)/shard_map/slice | solution.py:107
  223.3 1.8 multiply_convert_fusion.1
  225.1 1.9 fusion.17
  227.1 3.1 collective-permute-start
  230.2 3.4 collective-permute-start.2
  233.6 8.7 %collective-permute-done = bf16[256,768]{1,0:T(8,128)(2,1)} collective-permute-done((bf16[256,768]{1,0:T(8,128)(2,1)}, bf16[256,768]{1,0:T(8,128)(2,1)}, u32[]{:S(2)}, u32[]{:S(2)}) %collective-permute-start) | collective-permute-done | bytes 393248 | tf_op jit(solution)/shard_map/ppermute | solution.py:20
  242.2 2.9 collective-permute-start.1
  245.1 1.4 fusion.39
  246.5 2.3 squeeze.14
  248.8 1.1 squeeze.15
  249.9 12.0 %collective-permute-done.1 = bf16[256,768]{1,0:T(8,128)(2,1)} collective-permute-done((bf16[256,768]{1,0:T(8,128)(2,1)}, bf16[256,768]{1,0:T(8,128)(2,1)}, u32[]{:S(2)}, u32[]{:S(2)}) %collective-permute-start.1) | collective-permute-done | bytes 393248 | tf_op jit(solution)/shard_map/ppermute | solution.py:20
  261.8 1.5 pad_maximum_fusion
  263.4 1.8 gather_fusion
  265.2 2.6 fusion.40
  267.8 2.0 add_convert_fusion.1
  269.8 3.5 all-to-all-start.3
  273.3 1.5 reshape_reshape.3
  274.8 2.4 copy.31
  277.2 10.0 %all-to-all-done.3 = bf16[4,256,512]{2,1,0:T(8,128)(2,1)S(1)} async-done(((bf16[4,256,512]{2,1,0:T(8,128)(2,1)}), bf16[4,256,512]{2,1,0:T(8,128)(2,1)S(1)}, u32[]{:S(2)}, u32[]{:S(2)}) %all-to-all-start.3) | async-done | bytes 1048608 | tf_op jit(solution)/shard_map/all_to_all | solution.py:141
  287.2 1.0 copy-done.4
  288.2 3.5 all-to-all-start.5
  291.7 2.0 copy.30
  293.8 1.2 reshape.128
  295.0 9.8 %all-to-all-done.5 = bf16[256,4,512]{2,0,1:T(8,128)(2,1)S(1)} async-done(((bf16[256,4,512]{2,0,1:T(8,128)(2,1)}), bf16[256,4,512]{2,0,1:T(8,128)(2,1)S(1)}, u32[]{:S(2)}, u32[]{:S(2)}) %all-to-all-start.5) | async-done | bytes 1048608 | tf_op jit(solution)/shard_map/all_to_all | solution.py:118
  304.8 13.0 %all-to-all-start.4 = ((bf16[128,2,2048]{2,1,0:T(2,128)(2,1)}), bf16[128,2,2048]{2,1,0:T(2,128)(2,1)}, u32[]{:S(2)}, u32[]{:S(2)}) async-start(bf16[128,2,2048]{2,1,0:T(2,128)(2,1)} %reshape.128), calls=%async_computation.4 | async-start | bytes 2097152 | tf_op jit(solution)/shard_map/all_to_all | solution.py:148
  322.3 2.0 add_convert_fusion
  324.2 2.9 convert_element_type.82
  327.1 1.7 copy.32
  328.9 44.1 %all-to-all-done.4 = bf16[128,2,2048]{2,1,0:T(2,128)(2,1)} async-done(((bf16[128,2,2048]{2,1,0:T(2,128)(2,1)}), bf16[128,2,2048]{2,1,0:T(2,128)(2,1)}, u32[]{:S(2)}, u32[]{:S(2)}) %all-to-all-start.4) | async-done | bytes 1048608 | tf_op jit(solution)/shard_map/all_to_all | solution.py:148
  373.0 6.5 %all-to-all-start.6 = ((bf16[2,128,4,768]{3,2,0,1:T(4,128)(2,1)}), bf16[2,128,4,768]{3,2,0,1:T(4,128)(2,1)S(1)}, u32[]{:S(2)}, u32[]{:S(2)}) async-start(bf16[2,128,4,768]{3,2,0,1:T(4,128)(2,1)} %copy.32), calls=%async_computation.6 | async-start | bytes 3145728 | tf_op jit(solution)/shard_map/all_to_all | solution.py:133
  379.5 1.5 reshape.129
  381.0 1.1 convolution_convert_fusion.1
  382.1 74.9 %all-to-all-done.6 = bf16[2,128,4,768]{3,2,0,1:T(4,128)(2,1)S(1)} async-done(((bf16[2,128,4,768]{3,2,0,1:T(4,128)(2,1)}), bf16[2,128,4,768]{3,2,0,1:T(4,128)(2,1)S(1)}, u32[]{:S(2)}, u32[]{:S(2)}) %all-to-all-start.6) | async-done | bytes 1572896 | tf_op jit(solution)/shard_map/all_to_all | solution.py:133
  457.5 1.5 copy.34
  (53 shorter events, 6.7 us)
Async XLA Ops:
  7.2 1.1 copy-start
  7.2 203.4 %all-gather.3.cloned.1.call-start = ((), (), s32[]{:S(2)}) async-start(), calls=%async_computation.7 | async-start | bytes 7864320 | tf_op jit(solution)/shard_map/all_gather | solution.py:106
  110.0 0.7 copy-start.11
  110.0 1.1 copy-start.10
  110.0 1.1 copy-start.13
  112.3 35.2 %all-to-all-start = ((bf16[128,2,768]{2,1,0:T(2,128)(2,1)}), bf16[128,2,768]{2,1,0:T(2,128)(2,1)S(1)}, u32[]{:S(2)}, u32[]{:S(2)}) async-start(bf16[128,2,768]{2,1,0:T(2,128)(2,1)} %reshape.122), calls=%async_computation | async-start | bytes 786432 | tf_op jit(solution)/shard_map/all_to_all | solution.py:87
  147.5 61.7 %all-to-all-start.1 = ((bf16[128,2,2048]{2,1,0:T(2,128)(2,1)}), bf16[128,2,2048]{2,1,0:T(2,128)(2,1)S(1)}, u32[]{:S(2)}, u32[]{:S(2)}) async-start(bf16[128,2,2048]{2,1,0:T(2,128)(2,1)} %reshape.123), calls=%async_computation.1 | async-start | bytes 2097152 | tf_op jit(solution)/shard_map/all_to_all | solution.py:80
  153.7 111.5 %all-gather.5.cloned.1.call-start = ((), (), s32[]{:S(2)}) async-start(), calls=%async_computation.8 | async-start | bytes 1966080 | tf_op jit(solution)/shard_map/all_gather | solution.py:114
  210.5 12.8 %copy-start.9 = (f32[256,768]{1,0:T(8,128)S(1)}, f32[256,768]{1,0:T(8,128)}, u32[]{:S(2)}) copy-start(f32[256,768]{1,0:T(8,128)} %reshape.130) | copy-start | bytes 2359300
  210.5 12.8 %copy-start.6 = (bf16[256,2048]{1,0:T(8,128)(2,1)S(1)}, bf16[256,2048]{1,0:T(8,128)(2,1)}, u32[]{:S(2)}) copy-start(bf16[256,2048]{1,0:T(8,128)(2,1)} %reshape.124) | copy-start | bytes 3145732
  227.1 15.2 %collective-permute-start = (bf16[256,768]{1,0:T(8,128)(2,1)}, bf16[256,768]{1,0:T(8,128)(2,1)}, u32[]{:S(2)}, u32[]{:S(2)}) collective-permute-start(bf16[256,768]{1,0:T(8,128)(2,1)} %get-tuple-element.14), channel_id=1, source_target_pairs={{0,128},{128,256},{256,384},{384,0},{1,129},{129,257},{257,385},{3... | collective-permute-start | bytes 1179656 | tf_op jit(solution)/shard_map/ppermute | solution.py:20
  230.2 19.7 %collective-permute-start.2 = (bf16[256,768]{1,0:T(8,128)(2,1)}, bf16[256,768]{1,0:T(8,128)(2,1)}, u32[]{:S(2)}, u32[]{:S(2)}) collective-permute-start(bf16[256,768]{1,0:T(8,128)(2,1)} %get-tuple-element.14), channel_id=1, source_target_pairs={{128,0},{256,128},{384,256},{0,384},{129,1},{257,129},{385,257},{1... | collective-permute-start | bytes 1179656 | tf_op jit(solution)/shard_map/ppermute | solution.py:22
  242.2 19.6 %collective-permute-start.1 = (bf16[256,768]{1,0:T(8,128)(2,1)}, bf16[256,768]{1,0:T(8,128)(2,1)}, u32[]{:S(2)}, u32[]{:S(2)}) collective-permute-start(bf16[256,768]{1,0:T(8,128)(2,1)} %collective-permute-done), channel_id=1, source_target_pairs={{0,128},{128,256},{256,384},{384,0},{1,129},{129,257},{257,385},{3... | collective-permute-start | bytes 1179656 | tf_op jit(solution)/shard_map/ppermute | solution.py:20
  263.4 1.8 copy-start.7
  265.2 2.6 copy-start.2
  265.2 2.6 copy-start.8
  269.8 17.4 %all-to-all-start.3 = ((bf16[4,256,512]{2,1,0:T(8,128)(2,1)}), bf16[4,256,512]{2,1,0:T(8,128)(2,1)S(1)}, u32[]{:S(2)}, u32[]{:S(2)}) async-start(bf16[4,256,512]{2,1,0:T(8,128)(2,1)} %bitcast.119), calls=%async_computation.3 | async-start | bytes 2097152 | tf_op jit(solution)/shard_map/all_to_all | solution.py:141
  287.2 1.0 copy-start.4
  288.2 16.6 %all-to-all-start.5 = ((bf16[256,4,512]{2,0,1:T(8,128)(2,1)}), bf16[256,4,512]{2,0,1:T(8,128)(2,1)S(1)}, u32[]{:S(2)}, u32[]{:S(2)}) async-start(bf16[256,4,512]{2,0,1:T(8,128)(2,1)} %copy.31), calls=%async_computation.5 | async-start | bytes 2097152 | tf_op jit(solution)/shard_map/all_to_all | solution.py:118
  295.0 22.8 %copy-start.3 = (bf16[4,256,768]{2,1,0:T(8,128)(2,1)S(1)}, bf16[4,256,768]{2,1,0:T(8,128)(2,1)}, u32[]{:S(2)}) copy-start(bf16[4,256,768]{2,1,0:T(8,128)(2,1)} %gather_fusion) | copy-start | bytes 4718596
  304.8 68.2 %all-to-all-start.4 = ((bf16[128,2,2048]{2,1,0:T(2,128)(2,1)}), bf16[128,2,2048]{2,1,0:T(2,128)(2,1)}, u32[]{:S(2)}, u32[]{:S(2)}) async-start(bf16[128,2,2048]{2,1,0:T(2,128)(2,1)} %reshape.128), calls=%async_computation.4 | async-start | bytes 2097152 | tf_op jit(solution)/shard_map/all_to_all | solution.py:148
  318.6 1.4 copy-start.5
  373.0 84.0 %all-to-all-start.6 = ((bf16[2,128,4,768]{3,2,0,1:T(4,128)(2,1)}), bf16[2,128,4,768]{3,2,0,1:T(4,128)(2,1)S(1)}, u32[]{:S(2)}, u32[]{:S(2)}) async-start(bf16[2,128,4,768]{3,2,0,1:T(4,128)(2,1)} %copy.32), calls=%async_computation.6 | async-start | bytes 3145728 | tf_op jit(solution)/shard_map/all_to_all | solution.py:133
  379.5 77.5 %copy-start.12 = (s32[128]{0:T(128)S(1)}, s32[128]{0:T(128)}, u32[]{:S(2)}) copy-start(s32[128]{0:T(128)} %param.10) | copy-start | bytes 1540
  381.0 78.0 %copy-start.1 = (bf16[64,2,4,768]{3,2,1,0:T(4,128)(2,1)S(1)}, bf16[64,2,4,768]{3,2,1,0:T(4,128)(2,1)}, u32[]{:S(2)}) copy-start(bf16[64,2,4,768]{3,2,1,0:T(4,128)(2,1)} %param.11) | copy-start | bytes 2359300
Sparse Core Ops, SparseCore 0:
  110.1 64.8 all-gather.2
  227.2 31.6 all-gather.4
